TPU v7x, 32 devices: a whole 2x2x4 slice. The times are simulated.
32 devices in a mesh: box: 16 (over z, x, core), shift: 2 (over y).
Axes of the slice: x: 2, y: 2, z: 4, core: 2. Of those that a mesh axis runs over, the one named last changes fastest.
Arguments:
- vectors: bfloat16 [2, 1024, 128, 128], P('shift', 'box'), may hold values from -6 to 6
- sigma: float32 [2, 2], P('shift'), may hold values from 0.5 to 2
- near_blocks: bfloat16 [1024, 6, 128, 128], P('box', None, 'shift'), may hold values from -0.21875 to 0.21875
- near_index: int32 [1024, 6], P('box'), may hold values from -1 to 1023, as said below
- radiate: bfloat16 [128, 128], replicated, may hold values from -0.5 to 0.5
- interp_one: bfloat16 [8, 512, 128], replicated, may hold values from -0.1875 to 0.1875
- interp_two: bfloat16 [8, 2048, 512], replicated, may hold values from -0.09375 to 0.09375
- trans_one: float32 [316, 512], replicated, may hold values from -1.5 to 1.5
- level1_source: int32 [128, 16], P('box'), may hold values from -1 to 127, as said below
- level1_offset: int32 [128, 16], P('box'), may hold values from 0 to 315
- trans_two: float32 [316, 2048], P(None, 'box'), may hold values from -1 to 1
- level2_source: int32 [16, 32], replicated, may hold values from -1 to 15, as said below
- level2_offset: int32 [16, 32], replicated, may hold values from 0 to 315
Outputs:
- applied: float32 [2, 1024, 128, 128], P('shift', 'box')
Inputs may be any that keep to these rules, and one draw needn't show every extreme that they name: `near_index`: leaf boxes are numbered along a space-filling curve. Entry 0 of each row is the box itself; every live entry names a box within 64 of the row's box; live entries come first, unused ones are -1; some rows use all 6 entries and some only one. `level1_source`: entry 0 of each row is live; every live entry names a box within 8 of the row's box; live entries come first, unused ones are -1; some rows use all 16 entries and some only one. `level2_source`: entry 0 of each row is live; live entries come first, unused ones are -1; some rows use all 32 entries and some only one.
All inputs are finite; a program needn't handle non-finite values.
Results may differ from a plain program's by a relative error of at most 0.0035.
Values may be sent and summed in bfloat16 or wider, within the bound.
No kernel may reach another device: no remote copies, remote signals or barrier semaphores. Data moves between devices by JAX's collectives and lax.ppermute only.
A program may use at most 192 MiB of HBM per device.

v0:
```python
import jax
import jax.numpy as jnp
from jax import lax
from jax.sharding import PartitionSpec as P


def extended(block, sides, width):
    for axis, dim in sides:
        count = lax.axis_size(axis)
        forward = [(i, i + 1) for i in range(count - 1)]
        backward = [(target, source) for source, target in forward]
        low = lax.ppermute(
            lax.slice_in_dim(block, block.shape[dim] - width, None, axis=dim), axis, forward
        )
        high = lax.ppermute(lax.slice_in_dim(block, 0, width, axis=dim), axis, backward)
        block = jnp.concatenate([low, block, high], axis=dim)
    return block


def weighted_lists(pattern, table, offsets, sources, base):
    live = sources >= 0
    local = jnp.where(live, sources - base, 0)
    weights = table[offsets] * live[:, :, None].astype(jnp.float32)
    picked = pattern[local]
    return jnp.einsum("cjk,cjkr->ckr", weights, picked, preferred_element_type=jnp.float32)


def body(
    vectors,
    sigma,
    near_blocks,
    near_index,
    radiate,
    interp_one,
    interp_two,
    trans_one,
    level1_source,
    level1_offset,
    trans_two,
    level2_source,
    level2_offset,
):
    box_count = vectors.shape[1]
    unknowns = vectors.shape[2]
    columns = vectors.shape[3]
    samples0 = radiate.shape[0]
    samples1 = interp_one.shape[1]
    my_box = lax.axis_index("box")
    live = near_index >= 0
    local = jnp.where(live, near_index - (my_box * box_count - box_count), 0)
    live_mask = live[:, :, None, None].astype(jnp.bfloat16)
    haloed = extended(vectors, (("box", 1),), box_count)[0]
    near_source = haloed[local] * live_mask
    near = jnp.einsum(
        "bjvu,bjur->bvr",
        lax.all_gather(near_blocks, "shift", axis=2, tiled=True),
        near_source,
        preferred_element_type=jnp.float32,
    )
    field = vectors[0]
    leaf = jnp.einsum("ku,bur->bkr", radiate, field, preferred_element_type=jnp.float32).astype(
        jnp.bfloat16
    )
    upper = jnp.einsum(
        "oqk,cokr->cqr",
        interp_one,
        leaf.reshape(box_count // 8, 8, samples0, columns),
        preferred_element_type=jnp.float32,
    ).astype(jnp.bfloat16)
    coarse = jnp.einsum(
        "oqk,gokr->gqr",
        interp_two,
        upper.reshape(box_count // 64, 8, samples1, columns),
        preferred_element_type=jnp.float32,
    ).astype(jnp.bfloat16)
    turned = weighted_lists(
        lax.all_to_all(coarse, "box", split_axis=1, concat_axis=0, tiled=True),
        trans_two,
        level2_offset,
        level2_source,
        0,
    ).astype(jnp.bfloat16)
    incoming = lax.all_to_all(turned, "box", split_axis=0, concat_axis=1, tiled=True)
    parents = box_count // 8
    upper_rim = extended(upper, (("box", 0),), parents)
    across = weighted_lists(
        upper_rim, trans_one, level1_offset, level1_source, my_box * parents - parents
    )
    down = jnp.einsum(
        "oqk,gqr->gokr", interp_two, incoming, preferred_element_type=jnp.float32
    ).reshape(parents, samples1, columns)
    local_in = (across + down).astype(jnp.bfloat16)
    leaf_in = (
        jnp.einsum("oqk,cqr->cokr", interp_one, local_in, preferred_element_type=jnp.float32)
        .reshape(box_count, samples0, columns)
        .astype(jnp.bfloat16)
    )
    far = jnp.einsum("ku,bkr->bur", radiate, leaf_in, preferred_element_type=jnp.float32)
    real_part = field[:, : unknowns // 2].astype(jnp.float32)
    imag_part = field[:, unknowns // 2 :].astype(jnp.float32)
    sig_re = sigma[0, 0]
    sig_im = sigma[0, 1]
    scaled = jnp.concatenate(
        [sig_re * real_part - sig_im * imag_part, sig_re * imag_part + sig_im * real_part], axis=1
    )
    return (near + far - scaled)[None]


def solution(mesh):
    in_specs = (
        P("shift", "box", None, None),
        P("shift", None),
        P("box", None, "shift", None),
        P("box", None),
        P(),
        P(),
        P(),
        P(),
        P("box", None),
        P("box", None),
        P(None, "box"),
        P(),
        P(),
    )
    out_specs = P("shift", "box", None, None)
    return jax.shard_map(body, mesh=mesh, in_specs=in_specs, out_specs=out_specs, check_vma=False)
```

profile of v0, /device:TPU:0, one launch (start us, length us, event | category | flops | bytes accessed | tf_op | source)
XLA Modules:
  0.0 232.8 jit_solution(10471339703910101869)
XLA Ops:
  7.4 2.3 %fusion.13 = bf16[64,128,128]{2,1,0:T(8,128)(2,1)S(1)} fusion(bf16[1,64,128,128]{3,2,1,0:T(8,128)(2,1)} %param.13, bf16[128,128]{1,0:T(8,128)(2,1)S(1)} %copy-done.5), kind=kOutput, calls=%fused_computation.29 | convolution fusion | flops 269484032 | bytes 4227072 | tf_op jit(solution)/shard_map/ku,bur->bkr/dot_general | solution.py:61
  9.7 2.3 fusion.16
  12.0 3.4 %collective-permute-start.2 = (bf16[8,512,128]{1,2,0:T(8,128)(2,1)}, bf16[8,512,128]{1,2,0:T(8,128)(2,1)}, u32[]{:S(2)}, u32[]{:S(2)}) collective-permute-start(bf16[8,512,128]{1,2,0:T(8,128)(2,1)} %fusion.16), channel_id=1, source_target_pairs={{0,2},{2,4},{4,6},{6,8},{8,10},{10,12},{12,14},{14,16},{16,18},{18... | collective-permute-start | bytes 3145736 | tf_op jit(solution)/shard_map/ppermute | solution.py:12
  16.7 5.6 %collective-permute-start = (bf16[1,64,128,128]{3,2,1,0:T(8,128)(2,1)}, bf16[1,64,128,128]{3,2,1,0:T(8,128)(2,1)}, u32[]{:S(2)}, u32[]{:S(2)}) collective-permute-start(bf16[1,64,128,128]{3,2,1,0:T(8,128)(2,1)} %param.13), channel_id=1, source_target_pairs={{0,2},{2,4},{4,6},{6,8},{8,10},{10,12},{12,14},{14,16},{16,18},{18... | collective-permute-start | bytes 6291464 | tf_op jit(solution)/shard_map/ppermute | solution.py:12
  23.6 13.4 %fusion.7 = bf16[1,2048,128]{1,2,0:T(8,128)(2,1)S(1)} fusion(bf16[8,512,128]{1,2,0:T(8,128)(2,1)} %fusion.16, bf16[8,2048,512]{2,1,0:T(8,128)(2,1)} %param.19), kind=kOutput, calls=%fused_computation.23 | convolution fusion | flops 2147745792 | bytes 18350080 | tf_op jit(solution)/shard_map/oqk,gokr->gqr/dot_general | solution.py:70
  38.3 11.5 %reduce.4 = bf16[2048,128]{1,0:T(8,128)(2,1)S(1)} reduce(bf16[2048,1,128]{2,1,0:T(2,128)(2,1)S(1)} %bitcast.102, bf16[]{:T(256)} %broadcast.53), dimensions={1}, to_apply=%bitcast.88.reduce_sub_computation | reduce | bytes 1048578
  50.8 7.6 %all-to-all-start = ((bf16[16,2,8192]{2,1,0:T(2,128)(2,1)}), bf16[16,2,8192]{2,1,0:T(2,128)(2,1)}, u32[]{:S(2)}, u32[]{:S(2)}) async-start(bf16[16,2,8192]{2,1,0:T(2,128)(2,1)} %reshape.95), calls=%async_computation | async-start | bytes 1048576 | tf_op jit(solution)/shard_map/all_to_all | solution.py:77
  59.7 3.2 %copy.34 = bf16[1,64,128,128]{2,3,1,0:T(8,128)(2,1)S(1)} copy(bf16[1,64,128,128]{3,2,1,0:T(8,128)(2,1)} %param.13) | data formatting | bytes 4194304 | tf_op args[0]
  63.1 2.7 %gather_fusion.1 = f32[128,512]{1,0:T(8,128)} fusion(f32[316,512]{1,0:T(8,128)} %param.20, s32[1024]{0:T(1024)S(1)} %pad_clamp_fusion.3), kind=kCustom, calls=%fused_computation.1 | custom fusion | bytes 524800 | tf_op jit(solution)/shard_map/gather | solution.py:23
  70.9 6.1 %fusion.3 = (f32[64,64,128]{1,2,0:T(8,128)}, f32[64,64,128]{1,2,0:T(8,128)}) fusion(f32[]{:T(128)} %bitcast.34, f32[]{:T(128)} %bitcast.33, bf16[64,128,128]{1,2,0:T(8,128)(2,1)S(1)} %bitcast.99), kind=kLoop, calls=%fused_computation.15 | loop fusion | flops 4194304 | bytes 6291464 | tf_op jit(solution)/shard_map/sub | solution.py:104
  77.0 2.2 reshape.96
  79.3 13.6 %gather_fusion.4 = bf16[512,128,128]{2,1,0:T(8,128)(2,1)} fusion(bf16[16,128,128]{2,1,0:T(8,128)(2,1)S(1)} %bitcast.97, s32[1024]{0:T(1024)S(1)} %pad_clamp_fusion), kind=kCustom, calls=%fused_computation.4 | custom fusion | bytes 33556480 | tf_op jit(solution)/shard_map/gather | solution.py:24
  93.0 11.4 %multiply_reduce_fusion = bf16[16,128,128]{2,1,0:T(8,128)(2,1)S(1)} fusion(f32[16,128,32]{1,2,0:T(8,128)S(1)} %copy-done.4, bf16[512,128,128]{2,1,0:T(8,128)(2,1)} %gather_fusion.4), kind=kLoop, calls=%fused_computation.5 | loop fusion | flops 24903680 | bytes 17563648
  105.4 20.4 %all-to-all-start.1 = ((bf16[16,128,128]{1,2,0:T(8,128)(2,1)}), bf16[16,128,128]{1,2,0:T(8,128)(2,1)}, u32[]{:S(2)}, u32[]{:S(2)}) async-start(bf16[16,128,128]{1,2,0:T(8,128)(2,1)} %copy.54), calls=%async_computation.1 | async-start | bytes 1048576 | tf_op jit(solution)/shard_map/all_to_all | solution.py:83
  125.8 3.3 %pad_maximum_fusion = bf16[24,512,128]{1,2,0:T(8,128)(2,1)} fusion(bf16[8,512,128]{1,2,0:T(8,128)(2,1)} %collective-permute-done.3, bf16[8,512,128]{1,2,0:T(8,128)(2,1)} %fusion.16, bf16[8,512,128]{1,2,0:T(8,128)(2,1)} %collective-permute-done.2), kind=kLoop, calls=%fused_computation.20 | loop fusion | flops 3145728 | bytes 6291456 | tf_op jit(solution)/shard_map/concatenate | solution.py:16
  129.0 10.1 %gather_fusion.2 = bf16[128,512,128]{1,2,0:T(8,128)(2,1)} fusion(bf16[24,512,128]{1,2,0:T(8,128)(2,1)} %pad_maximum_fusion, s32[1024]{0:T(1024)S(1)} %pad_clamp_fusion.2), kind=kCustom, calls=%fused_computation.2 | custom fusion | bytes 33554944 | tf_op jit(solution)/shard_map/gather | solution.py:24
  139.1 9.3 %multiply_reduce_fusion.1 = f32[8,512,128]{1,2,0:T(8,128)S(1)} fusion(f32[8,512,16]{1,2,0:T(8,128)S(1)} %copy-done.3, bf16[128,512,128]{1,2,0:T(8,128)(2,1)} %gather_fusion.2), kind=kLoop, calls=%fused_computation.6 | loop fusion | flops 24641536 | bytes 19136512 | tf_op jit(solution)/shard_map/cjk,cjkr->ckr/dot_general | solution.py:25
  152.7 10.8 %convolution_convert_fusion = bf16[8,128,8,128]{3,1,2,0:T(8,128)(2,1)} fusion(bf16[8,512,128]{2,1,0:T(8,128)(2,1)S(1)} %copy-done, f32[8,512,128]{1,2,0:T(8,128)S(1)} %multiply_reduce_fusion.1, bf16[2048,128,1]{0,1,2:T(8,128)(2,1)} %reshape.92, bf16[8,2048,512]{2,1,0:T(8,128)(2,1)} %param.19), kind=kOutput, calls=%fused_computation.30 | convolution fusion | flops 3223322624 | bytes 22544384 | tf_op jit(solution)/shard_map/oqk,cqr->cokr/dot_general | solution.py:94
  163.4 4.2 %fusion.20 = f32[64,128,128]{2,1,0:T(8,128)} fusion(bf16[64,128,128]{1,2,0:T(8,128)(2,1)} %bitcast.100, bf16[128,128]{1,0:T(8,128)(2,1)S(1)} %copy-done.5), kind=kOutput, calls=%fused_computation.37 | convolution fusion | flops 268435456 | bytes 6324224 | tf_op jit(solution)/shard_map/ku,bkr->bur/dot_general | solution.py:98
  167.7 6.0 %maximum_bitcast_fusion = bf16[192,128,128]{2,1,0:T(8,128)(2,1)} fusion(bf16[1,64,128,128]{3,2,1,0:T(8,128)(2,1)} %collective-permute-done.1, bf16[1,64,128,128]{3,2,1,0:T(8,128)(2,1)} %param.13, bf16[1,64,128,128]{3,2,1,0:T(8,128)(2,1)} %collective-permute-done), kind=kLoop, calls=%fused_computation.9 | loop fusion | flops 6291456 | bytes 12582912 | tf_op jit(solution)/shard_map/squeeze | solution.py:52
  173.7 13.9 %gather_fusion = bf16[384,128,128]{2,1,0:T(8,128)(2,1)} fusion(bf16[192,128,128]{2,1,0:T(8,128)(2,1)} %maximum_bitcast_fusion, s32[1024]{0:T(1024)S(1)} %pad_clamp_fusion.4), kind=kCustom, calls=%fused_computation | custom fusion | bytes 25167360 | tf_op jit(solution)/shard_map/gather | solution.py:53
  187.6 16.6 %copy.33 = bf16[64,6,128,128]{2,3,1,0:T(8,128)(2,1)} copy(bf16[64,6,128,128]{3,2,1,0:T(8,128)(2,1)} %bitcast.98) | data formatting | bytes 25165824 | tf_op jit(solution)/shard_map/gather | solution.py:53
  204.3 16.0 %fusion.5 = f32[1,64,128,128]{2,3,1,0:T(8,128)} fusion(f32[64,64,128]{1,2,0:T(8,128)} %get-tuple-element.6, f32[64,64,128]{1,2,0:T(8,128)} %get-tuple-element.5, f32[64,128,128]{2,1,0:T(8,128)} %fusion.20, bf16[64,6,128,128]{3,2,1,0:T(8,128)(2,1)} %all-gather.2.cloned.1.call-done, bf16[64,6,128,128]{2,3,1,0:T(8,128)(2,1)} %copy.33, bf16[64,6]{1,0:T(8,128)(2,1)S(1)} %copy.32), kind=kOutput, calls=%fused_computation.18 | convolution fusion | flops 1620049920 | bytes 37749504 | tf_op jit(solution)/shard_map/bjvu,bjur->bvr/dot_general | solution.py:54
  220.3 5.6 %copy.37 = f32[1,64,128,128]{3,2,1,0:T(8,128)} copy(f32[1,64,128,128]{2,3,1,0:T(8,128)} %fusion.5) | data formatting | bytes 8388608 | tf_op jit(solution)/shard_map/broadcast_in_dim | solution.py:106
  (66 shorter events, 17.5 us)
Async XLA Ops:
  6.5 3.2 %copy-start = (bf16[8,512,128]{2,1,0:T(8,128)(2,1)S(1)}, bf16[8,512,128]{2,1,0:T(8,128)(2,1)}, u32[]{:S(2)}) copy-start(bf16[8,512,128]{2,1,0:T(8,128)(2,1)} %param.18) | copy-start | bytes 3145732
  6.5 0.8 copy-start.5
  6.5 197.7 %all-gather.2.cloned.1.call-start = ((), (), s32[]{:S(2)}) async-start(), calls=%async_computation.2 | async-start | bytes 18874368 | tf_op jit(solution)/shard_map/all_gather | solution.py:56
  12.0 113.7 %collective-permute-start.2 = (bf16[8,512,128]{1,2,0:T(8,128)(2,1)}, bf16[8,512,128]{1,2,0:T(8,128)(2,1)}, u32[]{:S(2)}, u32[]{:S(2)}) collective-permute-start(bf16[8,512,128]{1,2,0:T(8,128)(2,1)} %fusion.16), channel_id=1, source_target_pairs={{0,2},{2,4},{4,6},{6,8},{8,10},{10,12},{12,14},{14,16},{16,18},{18... | collective-permute-start | bytes 3145736 | tf_op jit(solution)/shard_map/ppermute | solution.py:12
  15.4 110.4 %collective-permute-start.3 = (bf16[8,512,128]{1,2,0:T(8,128)(2,1)}, bf16[8,512,128]{1,2,0:T(8,128)(2,1)}, u32[]{:S(2)}, u32[]{:S(2)}) collective-permute-start(bf16[8,512,128]{1,2,0:T(8,128)(2,1)} %fusion.16), channel_id=1, source_target_pairs={{2,0},{4,2},{6,4},{8,6},{10,8},{12,10},{14,12},{16,14},{18,16},{20... | collective-permute-start | bytes 3145736 | tf_op jit(solution)/shard_map/ppermute | solution.py:15
  16.7 151.0 %collective-permute-start = (bf16[1,64,128,128]{3,2,1,0:T(8,128)(2,1)}, bf16[1,64,128,128]{3,2,1,0:T(8,128)(2,1)}, u32[]{:S(2)}, u32[]{:S(2)}) collective-permute-start(bf16[1,64,128,128]{3,2,1,0:T(8,128)(2,1)} %param.13), channel_id=1, source_target_pairs={{0,2},{2,4},{4,6},{6,8},{8,10},{10,12},{12,14},{14,16},{16,18},{18... | collective-permute-start | bytes 6291464 | tf_op jit(solution)/shard_map/ppermute | solution.py:12
  22.3 145.3 %collective-permute-start.1 = (bf16[1,64,128,128]{3,2,1,0:T(8,128)(2,1)}, bf16[1,64,128,128]{3,2,1,0:T(8,128)(2,1)}, u32[]{:S(2)}, u32[]{:S(2)}) collective-permute-start(bf16[1,64,128,128]{3,2,1,0:T(8,128)(2,1)} %param.13), channel_id=1, source_target_pairs={{2,0},{4,2},{6,4},{8,6},{10,8},{12,10},{14,12},{16,14},{18,16},{20... | collective-permute-start | bytes 6291464 | tf_op jit(solution)/shard_map/ppermute | solution.py:15
  37.0 21.4 %copy-start.8 = (s32[8,16]{1,0:T(8,128)S(1)}, s32[8,16]{1,0:T(8,128)}, u32[]{:S(2)}) copy-start(s32[8,16]{1,0:T(8,128)} %param.21) | copy-start | bytes 1540
  37.0 21.5 %copy-start.10 = (s32[8,16]{1,0:T(8,128)S(1)}, s32[8,16]{1,0:T(8,128)}, u32[]{:S(2)}) copy-start(s32[8,16]{1,0:T(8,128)} %param.22) | copy-start | bytes 1540
  37.0 21.6 %copy-start.6 = (s32[16,32]{1,0:T(8,128)S(1)}, s32[16,32]{1,0:T(8,128)}, u32[]{:S(2)}) copy-start(s32[16,32]{1,0:T(8,128)} %param.24) | copy-start | bytes 6148
  37.0 21.7 %copy-start.9 = (s32[16,32]{1,0:T(8,128)S(1)}, s32[16,32]{1,0:T(8,128)}, u32[]{:S(2)}) copy-start(s32[16,32]{1,0:T(8,128)} %param.25) | copy-start | bytes 6148
  37.0 21.7 %copy-start.7 = (s32[64,6]{0,1:T(8,128)S(1)}, s32[64,6]{0,1:T(8,128)}, u32[]{:S(2)}) copy-start(s32[64,6]{0,1:T(8,128)} %param.16) | copy-start | bytes 4612
  37.0 22.0 %copy-start.11 = (f32[1,2]{1,0:T(1,128)S(1)}, f32[1,2]{1,0:T(1,128)}, u32[]{:S(2)}) copy-start(f32[1,2]{1,0:T(1,128)} %param.14) | copy-start | bytes 28
  49.9 15.8 %copy-start.2 = (f32[316,128]{1,0:T(8,128)S(1)}, f32[316,128]{1,0:T(8,128)}, u32[]{:S(2)}) copy-start(f32[316,128]{1,0:T(8,128)} %param.23) | copy-start | bytes 485380
  50.8 26.2 %all-to-all-start = ((bf16[16,2,8192]{2,1,0:T(2,128)(2,1)}), bf16[16,2,8192]{2,1,0:T(2,128)(2,1)}, u32[]{:S(2)}, u32[]{:S(2)}) async-start(bf16[16,2,8192]{2,1,0:T(2,128)(2,1)} %reshape.95), calls=%async_computation | async-start | bytes 1048576 | tf_op jit(solution)/shard_map/all_to_all | solution.py:77
  79.3 13.7 %copy-start.4 = (f32[16,128,32]{1,2,0:T(8,128)S(1)}, f32[16,128,32]{1,2,0:T(8,128)}, u32[]{:S(2)}) copy-start(f32[16,128,32]{1,2,0:T(8,128)} %multiply_bitcast_fusion) | copy-start | bytes 786436
  105.4 43.0 %all-to-all-start.1 = ((bf16[16,128,128]{1,2,0:T(8,128)(2,1)}), bf16[16,128,128]{1,2,0:T(8,128)(2,1)}, u32[]{:S(2)}, u32[]{:S(2)}) async-start(bf16[16,128,128]{1,2,0:T(8,128)(2,1)} %copy.54), calls=%async_computation.1 | async-start | bytes 1048576 | tf_op jit(solution)/shard_map/all_to_all | solution.py:83
  129.0 10.1 %copy-start.3 = (f32[8,512,16]{1,2,0:T(8,128)S(1)}, f32[8,512,16]{1,2,0:T(8,128)}, u32[]{:S(2)}) copy-start(f32[8,512,16]{1,2,0:T(8,128)} %multiply_bitcast_fusion.1) | copy-start | bytes 786436
  204.3 21.6 %copy-start.1 = (bf16[8,512,128]{2,1,0:T(8,128)(2,1)S(1)}, bf16[8,512,128]{2,1,0:T(8,128)(2,1)}, u32[]{:S(2)}) copy-start(bf16[8,512,128]{2,1,0:T(8,128)(2,1)} %param.18) | copy-start | bytes 3145732
Sparse Core Ops, SparseCore 0:
  8.9 155.2 all-gather.1
where the time goes:
time: 234 us; the launch traced here: 233 us
  local copies, waits for them, and re-layouts  78.6 us (34%)
  other arithmetic  51.2 us (22%)
  matrix products  49.1 us (21%)
  starting transfers between devices  39.5 us (17%)
  between operations  13.7 us (6%)
    gather x2, local copies, waits for them, and re-layouts, body(): near_source = haloed[local] * live_mask  30.6 us
    unnamed x4, other arithmetic  26.4 us
    gather x2, local copies, waits for them, and re-layouts, weighted_lists(): picked = pattern[local]  23.7 us
    all_to_all x1, starting transfers between devices, body(): lax.all_to_all(turned, 'box', split_axis=0, concat_axis=1, tiled=True)  20.4 us
    dot_general x1, matrix products, body(): jnp.einsum('bjvu,bjur->bvr', lax.all_gather(near_blocks, 'shift', axis=2,...  16 us
    dot_general x1, matrix products, body(): jnp.einsum('oqk,gokr->gqr', interp_two, upper.reshape(box_count // 64, 8,...  13.4 us
    dot_general x1, matrix products, body(): jnp.einsum('oqk,cqr->cokr', interp_one, local_in, preferred_element_type=...  10.8 us
    dot_general x1, other arithmetic, weighted_lists(): jnp.einsum('cjk,cjkr->ckr', weights, picked, preferred_element_type=jnp.f...  9.27 us
  transfers between devices with their start and end apart: 7, of which 0 were waited for; matrix products, arithmetic and copies ran while one was open for 67% of the time, Pallas kernels for 0%

commit v1 on v0

--- a/solution.py
+++ b/solution.py
@@ -80,7 +80,9 @@
         level2_source,
         0,
     ).astype(jnp.bfloat16)
-    incoming = lax.all_to_all(turned, "box", split_axis=0, concat_axis=1, tiled=True)
+    cells = jnp.split(turned, lax.axis_size("box"), axis=0)
+    got = lax.all_to_all(jnp.stack(cells), "box", 0, 0)
+    incoming = jnp.concatenate(got, axis=1)
     parents = box_count // 8
     upper_rim = extended(upper, (("box", 0),), parents)
     across = weighted_lists(

time: 234 us -> 243 us (1.038)
  matrix products: 49.1 us -> 64.1 us
  other arithmetic: 51.2 us -> 37.5 us
  local copies, waits for them, and re-layouts: 78.6 us -> 84.3 us
  starting transfers between devices: 39.5 us -> 42.3 us
    dot_general x0 -> x1, matrix products: none -> 16.8 us  [weighted_lists(): jnp.einsum('cjk,cjkr->ckr', weights, picked, preferred_element_type=jnp.f...]
    unnamed x4 -> x2, other arithmetic: 26.4 us -> 12.6 us
    unnamed x29 -> x42, local copies, waits for them, and re-layouts: 7.13 us -> 16.1 us
  transfers between devices with their start and end apart: 7 -> 7, of which waited for: 0 -> 0; matrix products, arithmetic and copies ran while one was open for 67% -> 66% of each run, Pallas kernels for 0% -> 0%
where the time goes in v1:
time: 243 us; the launch traced here: 242 us
  local copies, waits for them, and re-layouts  84.3 us (35%)
  matrix products  64.1 us (26%)
  starting transfers between devices  42.3 us (17%)
  other arithmetic  37.5 us (15%)
  between operations  13.7 us (6%)
    gather x2, local copies, waits for them, and re-layouts, body(): near_source = haloed[local] * live_mask  30.6 us
    gather x2, local copies, waits for them, and re-layouts, weighted_lists(): picked = pattern[local]  23.7 us
    all_to_all x1, starting transfers between devices, body(): got = lax.all_to_all(jnp.stack(cells), 'box', 0, 0)  22.8 us
    dot_general x1, matrix products, weighted_lists(): jnp.einsum('cjk,cjkr->ckr', weights, picked, preferred_element_type=jnp.f...  16.8 us
    unnamed x42, local copies, waits for them, and re-layouts  16.1 us
    dot_general x1, matrix products, body(): jnp.einsum('bjvu,bjur->bvr', lax.all_gather(near_blocks, 'shift', axis=2,...  16 us
    unnamed x2, other arithmetic  12.6 us
    dot_general x1, matrix products, body(): jnp.einsum('oqk,gokr->gqr', interp_two, upper.reshape(box_count // 64, 8,...  11.5 us
  transfers between devices with their start and end apart: 7, of which 0 were waited for; matrix products, arithmetic and copies ran while one was open for 66% of the time, Pallas kernels for 0%

profile of v1, /device:TPU:0, one launch (start us, length us, event | category | flops | bytes accessed | tf_op | source)
XLA Modules:
  0.0 241.9 jit_solution(10915034410267981283)
XLA Ops:
  6.5 2.4 %fusion.15 = bf16[64,128,128]{2,1,0:T(8,128)(2,1)S(1)} fusion(bf16[1,64,128,128]{3,2,1,0:T(8,128)(2,1)} %param.13, bf16[128,128]{1,0:T(8,128)(2,1)} %param.17), kind=kOutput, calls=%fused_computation.30 | convolution fusion | flops 269484032 | bytes 4227072 | tf_op jit(solution)/shard_map/ku,bur->bkr/dot_general | solution.py:61
  9.0 2.3 fusion.18
  11.3 3.4 %collective-permute-start.2 = (bf16[8,512,128]{1,2,0:T(8,128)(2,1)}, bf16[8,512,128]{1,2,0:T(8,128)(2,1)}, u32[]{:S(2)}, u32[]{:S(2)}) collective-permute-start(bf16[8,512,128]{1,2,0:T(8,128)(2,1)} %fusion.18), channel_id=1, source_target_pairs={{0,2},{2,4},{4,6},{6,8},{8,10},{10,12},{12,14},{14,16},{16,18},{18... | collective-permute-start | bytes 3145736 | tf_op jit(solution)/shard_map/ppermute | solution.py:12
  15.9 5.5 %collective-permute-start = (bf16[1,64,128,128]{3,2,1,0:T(8,128)(2,1)}, bf16[1,64,128,128]{3,2,1,0:T(8,128)(2,1)}, u32[]{:S(2)}, u32[]{:S(2)}) collective-permute-start(bf16[1,64,128,128]{3,2,1,0:T(8,128)(2,1)} %param.13), channel_id=1, source_target_pairs={{0,2},{2,4},{4,6},{6,8},{8,10},{10,12},{12,14},{14,16},{16,18},{18... | collective-permute-start | bytes 6291464 | tf_op jit(solution)/shard_map/ppermute | solution.py:12
  22.7 11.5 %fusion.9 = bf16[1,2048,128]{1,2,0:T(8,128)(2,1)S(1)} fusion(bf16[8,512,128]{1,2,0:T(8,128)(2,1)} %fusion.18, bf16[8,2048,512]{2,1,0:T(8,128)(2,1)} %param.19), kind=kOutput, calls=%fused_computation.24 | convolution fusion | flops 2147745792 | bytes 18350080 | tf_op jit(solution)/shard_map/oqk,gokr->gqr/dot_general | solution.py:70
  35.6 11.5 %reduce.2 = bf16[2048,128]{1,0:T(8,128)(2,1)S(1)} reduce(bf16[2048,1,128]{2,1,0:T(2,128)(2,1)S(1)} %bitcast.169, bf16[]{:T(256)} %broadcast.52), dimensions={1}, to_apply=%bitcast.153.reduce_sub_computation | reduce | bytes 1048578
  48.1 8.1 %all-to-all-start = ((bf16[16,2,8192]{2,1,0:T(2,128)(2,1)}), bf16[16,2,8192]{2,1,0:T(2,128)(2,1)}, u32[]{:S(2)}, u32[]{:S(2)}) async-start(bf16[16,2,8192]{2,1,0:T(2,128)(2,1)} %reshape.92), calls=%async_computation | async-start | bytes 1048576 | tf_op jit(solution)/shard_map/all_to_all | solution.py:77
  58.7 3.2 %copy.50 = bf16[1,64,128,128]{2,3,1,0:T(8,128)(2,1)S(1)} copy(bf16[1,64,128,128]{3,2,1,0:T(8,128)(2,1)} %param.13) | data formatting | bytes 4194304 | tf_op args[0]
  64.0 2.7 %gather_fusion.1 = f32[128,512]{1,0:T(8,128)} fusion(f32[316,512]{1,0:T(8,128)} %param.20, s32[1024]{0:T(1024)S(1)} %pad_clamp_fusion.3), kind=kCustom, calls=%fused_computation.1 | custom fusion | bytes 524800 | tf_op jit(solution)/shard_map/gather | solution.py:23
  67.7 6.1 %fusion.5 = (f32[64,64,128]{1,2,0:T(8,128)}, f32[64,64,128]{1,2,0:T(8,128)}) fusion(f32[]{:T(128)} %bitcast.52, f32[]{:T(128)} %bitcast.51, bf16[64,128,128]{1,2,0:T(8,128)(2,1)S(1)} %bitcast.165), kind=kLoop, calls=%fused_computation.16 | loop fusion | flops 4194304 | bytes 6291464 | tf_op jit(solution)/shard_map/sub | solution.py:106
  73.9 2.2 reshape.93
  76.2 13.6 %gather_fusion.4 = bf16[512,128,128]{2,1,0:T(8,128)(2,1)} fusion(bf16[16,128,128]{2,1,0:T(8,128)(2,1)S(1)} %bitcast.163, s32[1024]{0:T(1024)S(1)} %get-tuple-element.9), kind=kCustom, calls=%fused_computation.4 | custom fusion | bytes 33556480 | tf_op jit(solution)/shard_map/gather | solution.py:24
  89.8 16.8 %fusion = f32[16,128,1,128]{3,2,1,0:T(1,128)S(1)} fusion(bf16[16,32,128,1]{1,3,2,0:T(2,128)(2,1)S(1)} %copy-done.3, bf16[16,32,128,128]{3,2,1,0:T(8,128)(2,1)} %bitcast.166), kind=kOutput, calls=%fused_computation.6 | convolution fusion | flops 16777216 | bytes 17956864 | tf_op jit(solution)/shard_map/cjk,cjkr->ckr/dot_general | solution.py:25
  116.4 22.8 %all-to-all-start.1 = ((bf16[16,1,128,128]{3,2,1,0:T(8,128)(2,1)}), bf16[16,1,128,128]{3,2,1,0:T(8,128)(2,1)}, u32[]{:S(2)}, u32[]{:S(2)}) async-start(bf16[16,1,128,128]{3,2,1,0:T(8,128)(2,1)} %fusion.22), calls=%async_computation.1 | async-start | bytes 1048576 | tf_op jit(solution)/shard_map/all_to_all | solution.py:84
  139.2 3.2 %pad_maximum_fusion = bf16[24,512,128]{1,2,0:T(8,128)(2,1)} fusion(bf16[8,512,128]{1,2,0:T(8,128)(2,1)} %collective-permute-done.3, bf16[8,512,128]{1,2,0:T(8,128)(2,1)} %fusion.18, bf16[8,512,128]{1,2,0:T(8,128)(2,1)} %collective-permute-done.2), kind=kLoop, calls=%fused_computation.21 | loop fusion | flops 3145728 | bytes 6291456 | tf_op jit(solution)/shard_map/concatenate | solution.py:16
  142.4 10.0 %gather_fusion.2 = bf16[128,512,128]{1,2,0:T(8,128)(2,1)} fusion(bf16[24,512,128]{1,2,0:T(8,128)(2,1)} %pad_maximum_fusion, s32[1024]{0:T(1024)S(1)} %pad_clamp_fusion.2), kind=kCustom, calls=%fused_computation.2 | custom fusion | bytes 33554944 | tf_op jit(solution)/shard_map/gather | solution.py:24
  152.5 9.3 %multiply_reduce_fusion = f32[8,512,128]{1,2,0:T(8,128)S(1)} fusion(f32[8,512,16]{1,2,0:T(8,128)S(1)} %multiply_bitcast_fusion.1, bf16[128,512,128]{1,2,0:T(8,128)(2,1)} %gather_fusion.2), kind=kLoop, calls=%fused_computation.5 | loop fusion | flops 24641536 | bytes 19136512 | tf_op jit(solution)/shard_map/cjk,cjkr->ckr/dot_general | solution.py:25
  161.8 10.8 %convolution_convert_fusion = bf16[8,128,8,128]{3,1,2,0:T(8,128)(2,1)} fusion(bf16[8,512,128]{2,1,0:T(8,128)(2,1)S(1)} %copy-done, f32[8,512,128]{1,2,0:T(8,128)S(1)} %multiply_reduce_fusion, bf16[2048,128,1]{1,0,2:T(8,128)(2,1)} %bitcast.62, bf16[8,2048,512]{2,1,0:T(8,128)(2,1)} %param.19), kind=kOutput, calls=%fused_computation.31 | convolution fusion | flops 3223322624 | bytes 22544384 | tf_op jit(solution)/shard_map/oqk,cqr->cokr/dot_general | solution.py:96
  172.6 4.2 %fusion.38 = f32[64,128,128]{2,1,0:T(8,128)} fusion(bf16[64,128,128]{1,2,0:T(8,128)(2,1)} %bitcast.167, bf16[128,128]{1,0:T(8,128)(2,1)S(1)} %copy-done.4), kind=kOutput, calls=%fused_computation.70 | convolution fusion | flops 268435456 | bytes 6324224 | tf_op jit(solution)/shard_map/ku,bkr->bur/dot_general | solution.py:100
  176.8 6.0 %maximum_bitcast_fusion = bf16[192,128,128]{2,1,0:T(8,128)(2,1)} fusion(bf16[1,64,128,128]{3,2,1,0:T(8,128)(2,1)} %collective-permute-done.1, bf16[1,64,128,128]{3,2,1,0:T(8,128)(2,1)} %param.13, bf16[1,64,128,128]{3,2,1,0:T(8,128)(2,1)} %collective-permute-done), kind=kLoop, calls=%fused_computation.10 | loop fusion | flops 6291456 | bytes 12582912 | tf_op jit(solution)/shard_map/squeeze | solution.py:52
  182.8 13.9 %gather_fusion = bf16[384,128,128]{2,1,0:T(8,128)(2,1)} fusion(bf16[192,128,128]{2,1,0:T(8,128)(2,1)} %maximum_bitcast_fusion, s32[1024]{0:T(1024)S(1)} %pad_clamp_fusion.4), kind=kCustom, calls=%fused_computation | custom fusion | bytes 25167360 | tf_op jit(solution)/shard_map/gather | solution.py:53
  196.8 16.6 %copy.49 = bf16[64,6,128,128]{2,3,1,0:T(8,128)(2,1)} copy(bf16[64,6,128,128]{3,2,1,0:T(8,128)(2,1)} %bitcast.164) | data formatting | bytes 25165824 | tf_op jit(solution)/shard_map/gather | solution.py:53
  213.4 16.0 %fusion.7 = f32[1,64,128,128]{2,3,1,0:T(8,128)} fusion(f32[64,64,128]{1,2,0:T(8,128)} %get-tuple-element.6, f32[64,64,128]{1,2,0:T(8,128)} %get-tuple-element.5, f32[64,128,128]{2,1,0:T(8,128)} %fusion.38, bf16[64,6,128,128]{3,2,1,0:T(8,128)(2,1)} %all-gather.2.cloned.1.call-done, bf16[64,6,128,128]{2,3,1,0:T(8,128)(2,1)} %copy.49, bf16[64,6]{1,0:T(8,128)(2,1)S(1)} %copy.48), kind=kOutput, calls=%fused_computation.19 | convolution fusion | flops 1620049920 | bytes 37749504 | tf_op jit(solution)/shard_map/bjvu,bjur->bvr/dot_general | solution.py:54
  229.4 5.6 %copy.53 = f32[1,64,128,128]{3,2,1,0:T(8,128)} copy(f32[1,64,128,128]{2,3,1,0:T(8,128)} %fusion.7) | data formatting | bytes 8388608 | tf_op jit(solution)/shard_map/broadcast_in_dim | solution.py:108
  (78 shorter events, 20.3 us)
Async XLA Ops:
  6.5 2.4 %copy-start = (bf16[8,512,128]{2,1,0:T(8,128)(2,1)S(1)}, bf16[8,512,128]{2,1,0:T(8,128)(2,1)}, u32[]{:S(2)}) copy-start(bf16[8,512,128]{2,1,0:T(8,128)(2,1)} %param.18) | copy-start | bytes 3145732
  6.5 206.9 %all-gather.2.cloned.1.call-start = ((), (), s32[]{:S(2)}) async-start(), calls=%async_computation.2 | async-start | bytes 18874368 | tf_op jit(solution)/shard_map/all_gather | solution.py:56
  11.3 127.9 %collective-permute-start.2 = (bf16[8,512,128]{1,2,0:T(8,128)(2,1)}, bf16[8,512,128]{1,2,0:T(8,128)(2,1)}, u32[]{:S(2)}, u32[]{:S(2)}) collective-permute-start(bf16[8,512,128]{1,2,0:T(8,128)(2,1)} %fusion.18), channel_id=1, source_target_pairs={{0,2},{2,4},{4,6},{6,8},{8,10},{10,12},{12,14},{14,16},{16,18},{18... | collective-permute-start | bytes 3145736 | tf_op jit(solution)/shard_map/ppermute | solution.py:12
  14.6 124.6 %collective-permute-start.3 = (bf16[8,512,128]{1,2,0:T(8,128)(2,1)}, bf16[8,512,128]{1,2,0:T(8,128)(2,1)}, u32[]{:S(2)}, u32[]{:S(2)}) collective-permute-start(bf16[8,512,128]{1,2,0:T(8,128)(2,1)} %fusion.18), channel_id=1, source_target_pairs={{2,0},{4,2},{6,4},{8,6},{10,8},{12,10},{14,12},{16,14},{18,16},{20... | collective-permute-start | bytes 3145736 | tf_op jit(solution)/shard_map/ppermute | solution.py:15
  15.9 160.9 %collective-permute-start = (bf16[1,64,128,128]{3,2,1,0:T(8,128)(2,1)}, bf16[1,64,128,128]{3,2,1,0:T(8,128)(2,1)}, u32[]{:S(2)}, u32[]{:S(2)}) collective-permute-start(bf16[1,64,128,128]{3,2,1,0:T(8,128)(2,1)} %param.13), channel_id=1, source_target_pairs={{0,2},{2,4},{4,6},{6,8},{8,10},{10,12},{12,14},{14,16},{16,18},{18... | collective-permute-start | bytes 6291464 | tf_op jit(solution)/shard_map/ppermute | solution.py:12
  21.4 155.4 %collective-permute-start.1 = (bf16[1,64,128,128]{3,2,1,0:T(8,128)(2,1)}, bf16[1,64,128,128]{3,2,1,0:T(8,128)(2,1)}, u32[]{:S(2)}, u32[]{:S(2)}) collective-permute-start(bf16[1,64,128,128]{3,2,1,0:T(8,128)(2,1)} %param.13), channel_id=1, source_target_pairs={{2,0},{4,2},{6,4},{8,6},{10,8},{12,10},{14,12},{16,14},{18,16},{20... | collective-permute-start | bytes 6291464 | tf_op jit(solution)/shard_map/ppermute | solution.py:15
  34.2 22.0 %copy-start.8 = (s32[16,32]{1,0:T(8,128)S(1)}, s32[16,32]{1,0:T(8,128)}, u32[]{:S(2)}) copy-start(s32[16,32]{1,0:T(8,128)} %param.25) | copy-start | bytes 6148
  34.2 22.0 %copy-start.5 = (s32[16,32]{1,0:T(8,128)S(1)}, s32[16,32]{1,0:T(8,128)}, u32[]{:S(2)}) copy-start(s32[16,32]{1,0:T(8,128)} %param.24) | copy-start | bytes 6148
  34.2 22.1 %copy-start.7 = (s32[8,16]{1,0:T(8,128)S(1)}, s32[8,16]{1,0:T(8,128)}, u32[]{:S(2)}) copy-start(s32[8,16]{1,0:T(8,128)} %param.21) | copy-start | bytes 1540
  34.3 22.2 %copy-start.9 = (s32[8,16]{1,0:T(8,128)S(1)}, s32[8,16]{1,0:T(8,128)}, u32[]{:S(2)}) copy-start(s32[8,16]{1,0:T(8,128)} %param.22) | copy-start | bytes 1540
  34.3 22.3 %copy-start.6 = (s32[64,6]{0,1:T(8,128)S(1)}, s32[64,6]{0,1:T(8,128)}, u32[]{:S(2)}) copy-start(s32[64,6]{0,1:T(8,128)} %param.16) | copy-start | bytes 4612
  34.3 22.5 %copy-start.2 = (f32[316,128]{1,0:T(8,128)S(1)}, f32[316,128]{1,0:T(8,128)}, u32[]{:S(2)}) copy-start(f32[316,128]{1,0:T(8,128)} %param.23) | copy-start | bytes 485380
  34.3 23.6 %copy-start.10 = (f32[1,2]{1,0:T(1,128)S(1)}, f32[1,2]{1,0:T(1,128)}, u32[]{:S(2)}) copy-start(f32[1,2]{1,0:T(1,128)} %param.14) | copy-start | bytes 28
  48.1 25.8 %all-to-all-start = ((bf16[16,2,8192]{2,1,0:T(2,128)(2,1)}), bf16[16,2,8192]{2,1,0:T(2,128)(2,1)}, u32[]{:S(2)}, u32[]{:S(2)}) async-start(bf16[16,2,8192]{2,1,0:T(2,128)(2,1)} %reshape.92), calls=%async_computation | async-start | bytes 1048576 | tf_op jit(solution)/shard_map/all_to_all | solution.py:77
  76.2 13.6 %copy-start.3 = (bf16[16,32,128,1]{1,3,2,0:T(2,128)(2,1)S(1)}, bf16[16,32,128,1]{1,3,2,0:T(2,128)(2,1)}, u32[]{:S(2)}) copy-start(bf16[16,32,128,1]{1,3,2,0:T(2,128)(2,1)} %copy.63) | copy-start | bytes 393220
  116.4 45.3 %all-to-all-start.1 = ((bf16[16,1,128,128]{3,2,1,0:T(8,128)(2,1)}), bf16[16,1,128,128]{3,2,1,0:T(8,128)(2,1)}, u32[]{:S(2)}, u32[]{:S(2)}) async-start(bf16[16,1,128,128]{3,2,1,0:T(8,128)(2,1)} %fusion.22), calls=%async_computation.1 | async-start | bytes 1048576 | tf_op jit(solution)/shard_map/all_to_all | solution.py:84
  161.8 10.8 %copy-start.4 = (bf16[128,128]{1,0:T(8,128)(2,1)S(1)}, bf16[128,128]{1,0:T(8,128)(2,1)}, u32[]{:S(2)}) copy-start(bf16[128,128]{1,0:T(8,128)(2,1)} %param.17) | copy-start | bytes 98308
  213.4 21.6 %copy-start.1 = (bf16[8,512,128]{2,1,0:T(8,128)(2,1)S(1)}, bf16[8,512,128]{2,1,0:T(8,128)(2,1)}, u32[]{:S(2)}) copy-start(bf16[8,512,128]{2,1,0:T(8,128)(2,1)} %param.18) | copy-start | bytes 3145732
Sparse Core Ops, SparseCore 0:
  22.9 155.8 all-gather.1
